TPU v7x, 256 devices: a whole 4x4x8 slice. The times are simulated.
256 devices in a mesh: wide: 32 (over z_hi, x, core), narrow: 8 (over z_lo, y).
Axes of the slice: x: 4, y: 4, z: 8 (z_hi: 4, z_lo: 2; z = z_hi * 2 + z_lo), core: 2. Of those that a mesh axis runs over, the one named last changes fastest.
Arguments:
- resid: bfloat16 [1024, 5120], P('wide'), may hold values from -6 to 6
- final_gain: float32 [5120], replicated, may hold values from 0.25 to 1.75
- unembed: bfloat16 [16384, 5120], P('narrow', 'wide'), may hold values from -12 to 12
- labels: int32 [1024, 4], replicated, may hold values from 0 to 16383
- layer_in: bfloat16 [1024, 5120], P('wide'), may hold values from -6 to 6
- gate_value: bfloat16 [1024, 13824], P('wide', 'narrow'), may hold values from -0.29882812 to 2
- down_weight: bfloat16 [13824, 5120], P('narrow', 'wide'), may hold values from -0.078125 to 0.078125
- basis_in: bfloat16 [5120, 5120], P('wide', 'narrow'), may hold values from -0.078125 to 0.078125
- basis_out: bfloat16 [13824, 13824], P('narrow', 'wide'), may hold values from -0.0546875 to 0.0546875
Outputs:
- corrected: float32 [13824, 5120], P('wide', 'narrow')
All inputs are finite; a program needn't handle non-finite values.
Results may differ from a plain program's by a relative error of at most 0.002.
The roundings to bfloat16 on the way count: a program that leaves them out, or rounds other values in their place, can miss the bound.
Values may be sent and summed in bfloat16 or wider, within the bound.
A program may use at most 128 MiB of HBM per device.

v0:
```python
import jax
import jax.numpy as jnp
from jax import lax
from jax.sharding import PartitionSpec as P

SEQ = 256
EXAMPLES = 4
EPSILON = 1e-05


def sent_to_all(value, axis):
    copies = jnp.broadcast_to(value, (lax.axis_size(axis), *value.shape))
    return lax.all_to_all(copies, axis, split_axis=0, concat_axis=0, tiled=True)


def of_everyone(value, axis):
    return sent_to_all(value, axis).sum(axis=0)


def taken_together(value, axis):
    return sent_to_all(value, axis).max(axis=0)


def contract_last(left, right):
    return lax.dot_general(
        left, right, (((1,), (1,)), ((), ())), preferred_element_type=jnp.float32
    )


def per_device(
    resid, final_gain, unembed, labels, layer_in, gate_value, down_weight, basis_in, basis_out
):
    wide_count = lax.axis_size("wide")
    wide_place = lax.axis_index("wide")
    narrow_place = lax.axis_index("narrow")
    local_tokens, width = resid.shape
    all_tokens, samples = labels.shape
    column_part = width // wide_count
    vocab_part = unembed.shape[0]
    hidden_part = down_weight.shape[0]
    grad_rows = local_tokens * samples
    resid_cols, inputs_cols = (
        lax.all_to_all(resid, "wide", split_axis=1, concat_axis=0, tiled=True),
        lax.all_to_all(layer_in, "wide", split_axis=1, concat_axis=0, tiled=True),
    )
    resid_float = resid_cols.astype(jnp.float32)
    gain_cols = lax.dynamic_slice_in_dim(final_gain, wide_place * column_part, column_part, 0)
    square_sums = of_everyone(jnp.sum(resid_float * resid_float, axis=1), "wide")
    inverse = lax.rsqrt(square_sums / width + EPSILON)
    normed = (resid_float * inverse[:, None] * gain_cols).astype(jnp.bfloat16)
    logits = lax.psum_scatter(
        contract_last(normed, unembed), "wide", scatter_dimension=0, tiled=True
    )
    largest = taken_together(jnp.max(logits, axis=1), "narrow")
    scaled = jnp.exp(logits - largest[:, None])
    totals = of_everyone(jnp.sum(scaled, axis=1), "narrow")
    probs = (scaled / totals[:, None]).astype(jnp.bfloat16)
    common = jnp.dot(
        lax.all_gather(probs, "wide", axis=0, tiled=True),
        unembed,
        preferred_element_type=jnp.float32,
    )
    shifted = labels - narrow_place * vocab_part
    inside = ((shifted >= 0) & (shifted < vocab_part)).astype(jnp.float32)
    picked = (
        jnp.take(unembed, jnp.clip(shifted, 0, vocab_part - 1), axis=0).astype(jnp.float32)
        * inside[:, :, None]
    )
    label_part = (common[:, None, :] - picked).reshape(all_tokens * samples, column_part)
    label_grads = lax.psum(label_part, "narrow")
    grads_local = lax.all_to_all(
        label_grads, "wide", split_axis=0, concat_axis=1, tiled=True
    ).reshape(local_tokens, samples, width)
    resid_local = resid.astype(jnp.float32)
    inverse_local = lax.rsqrt(jnp.mean(resid_local * resid_local, axis=1) + EPSILON)
    inner = jnp.sum(final_gain * grads_local * resid_local[:, None, :], axis=2)
    back = (
        inverse_local[:, None, None] * final_gain * grads_local
        - resid_local[:, None, :] * (inverse_local**3)[:, None, None] * inner[:, :, None] / width
    )
    back = back.astype(jnp.bfloat16).reshape(grad_rows, width)
    hidden_grads = contract_last(back, lax.all_gather(down_weight, "wide", axis=1, tiled=True))
    gated = (
        hidden_grads.reshape(local_tokens, samples, hidden_part)
        * gate_value.astype(jnp.float32)[:, None, :]
    )
    gated = gated.astype(jnp.bfloat16).reshape(grad_rows, hidden_part)
    rotated_part = jnp.dot(
        lax.all_gather(gated, "wide", axis=0, tiled=True),
        basis_out,
        preferred_element_type=jnp.float32,
    )
    rotated = lax.psum(rotated_part, "narrow").astype(jnp.bfloat16)
    inputs_part = jnp.dot(inputs_cols, basis_in, preferred_element_type=jnp.float32)
    inputs_rot = lax.psum(inputs_part, "wide").astype(jnp.bfloat16)
    rot_blocks = rotated.reshape(EXAMPLES, SEQ, samples, rotated.shape[1])
    input_blocks = inputs_rot.reshape(EXAMPLES, SEQ, inputs_rot.shape[1])
    blocks = jnp.einsum(
        "etsj,etd->esjd", rot_blocks, input_blocks, preferred_element_type=jnp.float32
    )
    return jnp.mean(blocks * blocks, axis=(0, 1))


def solution(mesh):
    in_specs = (
        P("wide", None),
        P(),
        P("narrow", "wide"),
        P(),
        P("wide", None),
        P("wide", "narrow"),
        P("narrow", "wide"),
        P("wide", "narrow"),
        P("narrow", "wide"),
    )
    out_specs = P("wide", "narrow")
    return jax.shard_map(
        per_device, mesh=mesh, in_specs=in_specs, out_specs=out_specs, check_vma=False
    )
```

profile of v0, /device:TPU:70, one launch (start us, length us, event | category | flops | bytes accessed | tf_op | source)
XLA Modules:
  0.0 968.3 jit_solution(15569779703708332936)
XLA Ops:
  8.6 26.2 %all_to_all.66 = bf16[32,32,160]{2,0,1:T(8,128)(2,1)S(1)} all-to-all(bf16[32,32,160]{2,0,1:T(8,128)(2,1)S(1)} %copy.52), channel_id=1, replica_groups=mesh['wide'=32,'narrow'=8] {'wide'}, dimensions={1} | all-to-all | bytes 655360 | tf_op jit(solution)/shard_map/all_to_all | solution.py:43
  35.8 6.7 all-to-all-start.1
  42.6 6.6 all-to-all-done.1
  49.6 4.5 fusion.13
  54.1 119.5 %reduce-scatter.2.cloned.1.call-done = f32[32,2048]{1,0:T(8,128)} async-done(((f32[1024,2048]{1,0:T(8,128)}), f32[32,2048]{1,0:T(8,128)}) %reduce-scatter.2.cloned.1.call-update) | async-done | bytes 262160 | tf_op jit(solution)/shard_map/reduce_scatter | solution.py:51
  174.7 10.3 %all_to_all.67 = f32[8,1,32]{2,1,0:T(1,128)S(1)} all-to-all(f32[8,1,32]{2,1,0:T(1,128)S(1)} %broadcast_in_dim.41), channel_id=1, replica_groups=mesh['wide'=32,'narrow'=8] {'narrow'}, dimensions={0} | all-to-all | bytes 2048 | tf_op jit(solution)/shard_map/all_to_all | solution.py:13
  186.2 8.5 all_to_all.68
  202.4 16.9 %gather_fusion = bf16[4096,160]{1,0:T(8,128)(2,1)} fusion(bf16[2048,160]{1,0:T(8,128)(2,1)S(1)} %copy.59, s32[4096]{0:T(1024)S(1)} %broadcast_clamp_fusion), kind=kCustom, calls=%fused_computation | custom fusion | bytes 2637824 | tf_op jit(solution)/shard_map/jit(_take)/gather | solution.py:66
  219.4 34.8 %all-gather.4.cloned.1.call-done = bf16[1024,2048]{1,0:T(8,128)(2,1)} async-done(((bf16[32,2048]{1,0:T(8,128)(2,1)}), bf16[1024,2048]{1,0:T(8,128)(2,1)}) %all-gather.4.cloned.1.call-update) | async-done | bytes 4194320 | tf_op jit(solution)/shard_map/all_gather | solution.py:59
  254.2 3.5 fusion.14
  257.6 2.6 sub.32
  260.3 5.3 sub.33
  265.5 7.0 multiply_subtract_fusion
  272.5 5.1 copy.61
  278.2 89.5 %all-reduce.4.cloned.1.call-done = f32[32,128,160]{1,2,0:T(8,128)} async-done(((f32[32,128,160]{1,2,0:T(8,128)}), f32[32,128,160]{1,2,0:T(8,128)}) %all-reduce.4.cloned.1.call-update) | async-done | bytes 2621456 | tf_op jit(solution)/shard_map/psum | solution.py:70
  367.7 9.0 all-to-all-start.4
  377.0 2.1 mul.153
  379.1 5.7 mul.154
  386.8 58.8 %all-to-all-done.4 = f32[32,128,160]{1,2,0:T(8,128)} async-done(((f32[32,128,160]{1,2,0:T(8,128)}), f32[32,128,160]{1,2,0:T(8,128)}, u32[]{:S(2)}, u32[]{:S(2)}) %all-to-all-start.4) | async-done | bytes 2621472 | tf_op jit(solution)/shard_map/all_to_all | solution.py:71
  445.7 5.1 copy.62
  450.8 4.5 multiply_reduce_fusion.1
  455.4 5.8 reshape.127
  461.2 3.5 subtract_convert_fusion
  464.8 70.3 %all-gather.6.cloned.1.call-done = bf16[1728,5120]{0,1:T(8,128)(2,1)} async-done(((bf16[1728,160]{0,1:T(8,128)(2,1)}), bf16[1728,5120]{0,1:T(8,128)(2,1)}) %all-gather.6.cloned.1.call-update) | async-done | bytes 17694736 | tf_op jit(solution)/shard_map/all_gather | solution.py:82
  535.1 9.0 fusion.6
  546.5 36.9 %all_to_all.69 = bf16[32,32,160]{2,0,1:T(8,128)(2,1)S(1)} all-to-all(bf16[32,32,160]{2,0,1:T(8,128)(2,1)S(1)} %copy.66), channel_id=1, replica_groups=mesh['wide'=32,'narrow'=8] {'wide'}, dimensions={1} | all-to-all | bytes 655360 | tf_op jit(solution)/shard_map/all_to_all | solution.py:44
  585.4 192.2 %all-reduce.6 = bf16[1024,640]{1,0:T(8,128)(2,1)S(1)} all-reduce(f32[1024,640]{1,0:T(8,128)} %fusion.16), channel_id=1, replica_groups=mesh['wide'=32,'narrow'=8] {'wide'}, use_global_device_ids=true, to_apply=%region_11.12 | all-reduce | flops 655360 | bytes 3932160 | tf_op jit(solution)/shard_map/psum | solution.py:95
  777.7 11.7 %fusion.15 = f32[4096,432]{0,1:T(8,128)} fusion(bf16[4096,1728]{1,0:T(8,128)(2,1)} %all-gather.8.cloned.1.call-done, bf16[1728,432]{0,1:T(8,128)(2,1)S(1)} %copy-done), kind=kOutput, calls=%fused_computation.31 | convolution fusion | flops 6115295232 | bytes 22726656 | tf_op jit(solution)/shard_map/dot_general | solution.py:88
  789.4 152.2 %all-reduce.5 = bf16[4096,432]{0,1:T(8,128)(2,1)} all-reduce(f32[4096,432]{0,1:T(8,128)} %fusion.15), channel_id=1, replica_groups=mesh['wide'=32,'narrow'=8] {'narrow'}, use_global_device_ids=true, to_apply=%region_10.11 | all-reduce | flops 1769472 | bytes 10616832 | tf_op jit(solution)/shard_map/psum | solution.py:93
  941.7 6.4 copy.65
  948.1 7.0 reshape.129
  955.0 5.6 multiply_reduce_fusion
  (65 shorter events, 21.8 us)
Async XLA Ops:
  6.5 771.1 %copy-start = (bf16[1728,432]{0,1:T(8,128)(2,1)S(1)}, bf16[1728,432]{0,1:T(8,128)(2,1)}, u32[]{:S(2)}) copy-start(bf16[1728,432]{0,1:T(8,128)(2,1)} %param.17) | copy-start | bytes 4478980
  6.5 36.0 %copy-start.6 = (f32[5120]{0:T(1024)S(1)}, f32[5120]{0:T(1024)}, u32[]{:S(2)}) copy-start(f32[5120]{0:T(1024)} %param.10) | copy-start | bytes 61444
  6.5 43.0 %copy-start.2 = (bf16[2048,160]{0,1:T(8,128)(2,1)S(1)}, bf16[2048,160]{0,1:T(8,128)(2,1)}, u32[]{:S(2)}) copy-start(bf16[2048,160]{0,1:T(8,128)(2,1)} %param.11) | copy-start | bytes 1966084
  35.8 13.5 %all-to-all-start.1 = ((f32[32,1,1024]{2,1,0:T(1,128)}), f32[32,1,1024]{2,1,0:T(1,128)S(1)}, u32[]{:S(2)}, u32[]{:S(2)}) async-start(f32[32,1,1024]{2,1,0:T(1,128)} %broadcast_in_dim.40), calls=%async_computation.1 | async-start | bytes 262144 | tf_op jit(solution)/shard_map/all_to_all | solution.py:13
  42.5 131.2 %reduce-scatter.2.cloned.1.call-start = ((), (), s32[]{:S(2)}) async-start(), calls=%async_computation.7 | async-start | bytes 8650752 | tf_op jit(solution)/shard_map/reduce_scatter | solution.py:51
  54.1 143.0 %copy-start.7 = (s32[1024,4]{0,1:T(4,128)S(1)}, s32[1024,4]{0,1:T(4,128)}, u32[]{:S(2)}) copy-start(s32[1024,4]{0,1:T(4,128)} %param.12) | copy-start | bytes 49156
  54.1 200.1 %all-gather.4.cloned.1.call-start = ((), (), s32[]{:S(2)}) async-start(), calls=%async_computation.8 | async-start | bytes 4325376 | tf_op jit(solution)/shard_map/all_gather | solution.py:59
  196.5 171.2 %all-reduce.4.cloned.1.call-start = ((), (), s32[]{:S(2)}) async-start(), calls=%async_computation.9 | async-start | bytes 5242880 | tf_op jit(solution)/shard_map/psum | solution.py:70
  277.7 257.5 %all-gather.6.cloned.1.call-start = ((), (), s32[]{:S(2)}) async-start(), calls=%async_computation.10 | async-start | bytes 18923520 | tf_op jit(solution)/shard_map/all_gather | solution.py:82
  278.2 98.8 %copy-start.1 = (bf16[32,5120]{1,0:T(8,128)(2,1)S(1)}, bf16[32,5120]{1,0:T(8,128)(2,1)}, u32[]{:S(2)}) copy-start(bf16[32,5120]{1,0:T(8,128)(2,1)} %param.9) | copy-start | bytes 983044
  367.7 77.9 %all-to-all-start.4 = ((f32[32,128,160]{1,2,0:T(8,128)}), f32[32,128,160]{1,2,0:T(8,128)}, u32[]{:S(2)}, u32[]{:S(2)}) async-start(f32[32,128,160]{1,2,0:T(8,128)} %all-reduce.4.cloned.1.call-done), calls=%async_computation.5 | async-start | bytes 5242880 | tf_op jit(solution)/shard_map/all_to_all | solution.py:71
  376.7 400.9 %all-gather.8.cloned.1.call-start = ((), (), s32[]{:S(2)}) async-start(), calls=%async_computation.11 | async-start | bytes 15138816 | tf_op jit(solution)/shard_map/all_gather | solution.py:89
  379.1 5.7 copy-start.5
  464.8 80.8 %copy-start.3 = (bf16[32,5120]{1,0:T(8,128)(2,1)S(1)}, bf16[32,5120]{1,0:T(8,128)(2,1)}, u32[]{:S(2)}) copy-start(bf16[32,5120]{1,0:T(8,128)(2,1)} %param.13) | copy-start | bytes 983044
  544.2 39.2 %copy-start.4 = (bf16[160,640]{1,0:T(8,128)(2,1)S(1)}, bf16[160,640]{1,0:T(8,128)(2,1)}, u32[]{:S(2)}) copy-start(bf16[160,640]{1,0:T(8,128)(2,1)} %param.16) | copy-start | bytes 614404
Sparse Core Ops, SparseCore 0:
  54.2 119.3 reduce-scatter.1
  196.6 57.4 all-gather.3
  277.8 89.9 all-reduce.3
  370.1 164.9 all-gather.5
  545.6 118.2 all-gather.7
where the time goes:
time: 970 us; the launch traced here: 968 us
  blocking collectives  426 us (44%)
  waiting for transfers between devices  380 us (39%)
  local copies, waits for them, and re-layouts  73.3 us (8%)
  matrix products  36.3 us (4%)
  other arithmetic  22.6 us (2%)
  starting transfers between devices  16 us (2%)
  between operations  13.4 us (1%)
    psum x1, blocking collectives, per_device(): inputs_rot = lax.psum(inputs_part, 'wide').astype(jnp.bfloat16)  192 us
    psum x1, blocking collectives, per_device(): rotated = lax.psum(rotated_part, 'narrow').astype(jnp.bfloat16)  152 us
    reduce_scatter x1, waiting for transfers between devices, per_device(): lax.psum_scatter(contract_last(normed, unembed), 'wide', scatter_dimensio...  120 us
    psum x1, waiting for transfers between devices, per_device(): label_grads = lax.psum(label_part, 'narrow')  89.5 us
    all_gather x1, waiting for transfers between devices, per_device(): lax.all_gather(down_weight, 'wide', axis=1, tiled=True)  70.3 us
    all_to_all x1, waiting for transfers between devices, per_device(): lax.all_to_all(label_grads, 'wide', split_axis=0, concat_axis=1, tiled=True)  58.8 us
    all_to_all x1, blocking collectives, per_device(): lax.all_to_all(layer_in, 'wide', split_axis=1, concat_axis=0, tiled=True)  36.9 us
    all_gather x1, waiting for transfers between devices, per_device(): lax.all_gather(probs, 'wide', axis=0, tiled=True)  34.8 us
  transfers between devices with their start and end apart: 7, of which 6 were waited for; matrix products, arithmetic and copies ran while one was open for 6% of the time, Pallas kernels for 0%

commit v1 on v0

--- a/solution.py
+++ b/solution.py
@@ -67,7 +67,7 @@
         * inside[:, :, None]
     )
     label_part = (common[:, None, :] - picked).reshape(all_tokens * samples, column_part)
-    label_grads = lax.psum(label_part, "narrow")
+    label_grads = jnp.sum(jax.lax.all_gather(label_part, "narrow"), 0)
     grads_local = lax.all_to_all(
         label_grads, "wide", split_axis=0, concat_axis=1, tiled=True
     ).reshape(local_tokens, samples, width)

time: 970 us -> 1090 us (1.12)
  waiting for transfers between devices: 380 us -> 476 us
    all_gather x0 -> x1, waiting for transfers between devices: none -> 211 us  [per_device(): label_grads = jnp.sum(jax.lax.all_gather(label_part, 'narrow'), 0)]
    psum x1 -> x0, waiting for transfers between devices: 89.5 us -> none  [per_device(): label_grads = lax.psum(label_part, 'narrow')]
    all_gather x1, waiting for transfers between devices: 70.3 us -> 21.7 us  [per_device(): lax.all_gather(down_weight, 'wide', axis=1, tiled=True)]
    all_to_all x1, waiting for transfers between devices: 58.8 us -> 81.7 us  [per_device(): lax.all_to_all(label_grads, 'wide', split_axis=0, concat_axis=1, tiled=True)]
  transfers between devices with their start and end apart: 7 -> 7, of which waited for: 6 -> 6; matrix products, arithmetic and copies ran while one was open for 6% -> 7% of each run, Pallas kernels for 0% -> 0%
where the time goes in v1:
time: 1090 us; the launch traced here: 1080 us
  waiting for transfers between devices  476 us (44%)
  blocking collectives  424 us (39%)
  local copies, waits for them, and re-layouts  83.5 us (8%)
  matrix products  36.4 us (3%)
  other arithmetic  31.3 us (3%)
  starting transfers between devices  16.2 us (1%)
  between operations  13.4 us (1%)
    all_gather x1, waiting for transfers between devices, per_device(): label_grads = jnp.sum(jax.lax.all_gather(label_part, 'narrow'), 0)  211 us
    psum x1, blocking collectives, per_device(): inputs_rot = lax.psum(inputs_part, 'wide').astype(jnp.bfloat16)  201 us
    psum x1, blocking collectives, per_device(): rotated = lax.psum(rotated_part, 'narrow').astype(jnp.bfloat16)  146 us
    reduce_scatter x1, waiting for transfers between devices, per_device(): lax.psum_scatter(contract_last(normed, unembed), 'wide', scatter_dimensio...  120 us
    all_to_all x1, waiting for transfers between devices, per_device(): lax.all_to_all(label_grads, 'wide', split_axis=0, concat_axis=1, tiled=True)  81.7 us
    all_gather x1, waiting for transfers between devices, per_device(): lax.all_gather(probs, 'wide', axis=0, tiled=True)  34.8 us
    all_to_all x1, blocking collectives, per_device(): lax.all_to_all(layer_in, 'wide', split_axis=1, concat_axis=0, tiled=True)  33.1 us
    all_to_all x1, blocking collectives, per_device(): lax.all_to_all(resid, 'wide', split_axis=1, concat_axis=0, tiled=True)  26.2 us
  transfers between devices with their start and end apart: 7, of which 6 were waited for; matrix products, arithmetic and copies ran while one was open for 7% of the time, Pallas kernels for 0%

profile of v1, /device:TPU:70, one launch (start us, length us, event | category | flops | bytes accessed | tf_op | source)
XLA Modules:
  0.0 1081.0 jit_solution(15226141320428896597)
XLA Ops:
  8.6 26.2 %all_to_all.66 = bf16[32,32,160]{2,0,1:T(8,128)(2,1)S(1)} all-to-all(bf16[32,32,160]{2,0,1:T(8,128)(2,1)S(1)} %copy.84), channel_id=1, replica_groups=mesh['wide'=32,'narrow'=8] {'wide'}, dimensions={1} | all-to-all | bytes 655360 | tf_op jit(solution)/shard_map/all_to_all | solution.py:43
  35.8 6.7 all-to-all-start.1
  42.6 6.6 all-to-all-done.1
  49.6 4.5 fusion.13
  54.1 119.5 %reduce-scatter.2.cloned.1.call-done = f32[32,2048]{1,0:T(8,128)} async-done(((f32[1024,2048]{1,0:T(8,128)}), f32[32,2048]{1,0:T(8,128)}) %reduce-scatter.2.cloned.1.call-update) | async-done | bytes 262160 | tf_op jit(solution)/shard_map/reduce_scatter | solution.py:51
  174.7 10.3 all_to_all.67
  186.2 8.5 all_to_all.68
  202.4 16.9 %gather_fusion = bf16[4096,160]{1,0:T(8,128)(2,1)} fusion(bf16[2048,160]{1,0:T(8,128)(2,1)S(1)} %copy.91, s32[4096]{0:T(1024)S(1)} %broadcast_clamp_fusion), kind=kCustom, calls=%fused_computation | custom fusion | bytes 2637824 | tf_op jit(solution)/shard_map/jit(_take)/gather | solution.py:66
  219.4 34.8 %all-gather.5.cloned.1.call-done = bf16[1024,2048]{1,0:T(8,128)(2,1)} async-done(((bf16[32,2048]{1,0:T(8,128)(2,1)}), bf16[1024,2048]{1,0:T(8,128)(2,1)}) %all-gather.5.cloned.1.call-update) | async-done | bytes 4194320 | tf_op jit(solution)/shard_map/all_gather | solution.py:59
  254.2 3.5 fusion.14
  260.3 5.3 sub.39
  265.5 7.0 multiply_subtract_fusion
  272.5 5.1 copy.93
  278.2 211.0 %all-gather.7.cloned.1.call-done = f32[8,4096,160]{1,2,0:T(8,128)} async-done(((f32[1,4096,160]{1,2,0:T(8,128)}), f32[8,4096,160]{1,2,0:T(8,128)}) %all-gather.7.cloned.1.call-update) | async-done | bytes 20971536 | tf_op jit(solution)/shard_map/all_gather | solution.py:70
  489.2 9.5 reduce_sum.80
  498.6 4.9 copy.108
  503.5 5.3 copy.96
  508.8 9.2 all-to-all-start.4
  520.5 5.6 mul.160
  528.1 81.7 %all-to-all-done.4 = f32[32,128,160]{1,2,0:T(8,128)} async-done(((f32[32,128,160]{1,2,0:T(8,128)}), f32[32,128,160]{1,2,0:T(8,128)}, u32[]{:S(2)}, u32[]{:S(2)}) %all-to-all-start.4) | async-done | bytes 2621472 | tf_op jit(solution)/shard_map/all_to_all | solution.py:71
  609.8 5.1 copy.97
  614.9 4.5 multiply_reduce_fusion.1
  619.6 5.8 reshape.194
  628.2 21.7 %all-gather.9.cloned.1.call-done = bf16[1728,5120]{0,1:T(8,128)(2,1)} async-done(((bf16[1728,160]{0,1:T(8,128)(2,1)}), bf16[1728,5120]{0,1:T(8,128)(2,1)}) %all-gather.9.cloned.1.call-update) | async-done | bytes 17694736 | tf_op jit(solution)/shard_map/all_gather | solution.py:82
  649.8 9.0 fusion.6
  661.2 33.1 %all_to_all.69 = bf16[32,32,160]{2,0,1:T(8,128)(2,1)S(1)} all-to-all(bf16[32,32,160]{2,0,1:T(8,128)(2,1)S(1)} %copy.101), channel_id=1, replica_groups=mesh['wide'=32,'narrow'=8] {'wide'}, dimensions={1} | all-to-all | bytes 655360 | tf_op jit(solution)/shard_map/all_to_all | solution.py:44
  696.3 200.5 %all-reduce.3 = bf16[1024,640]{1,0:T(8,128)(2,1)S(1)} all-reduce(f32[1024,640]{1,0:T(8,128)} %fusion.16), channel_id=1, replica_groups=mesh['wide'=32,'narrow'=8] {'wide'}, use_global_device_ids=true, to_apply=%region_11.12 | all-reduce | flops 655360 | bytes 3932160 | tf_op jit(solution)/shard_map/psum | solution.py:95
  896.9 11.7 %fusion.15 = f32[4096,432]{0,1:T(8,128)} fusion(bf16[4096,1728]{1,0:T(8,128)(2,1)} %all-gather.11.cloned.1.call-done, bf16[1728,432]{0,1:T(8,128)(2,1)S(1)} %copy-done), kind=kOutput, calls=%fused_computation.32 | convolution fusion | flops 6115295232 | bytes 22726656 | tf_op jit(solution)/shard_map/dot_general | solution.py:88
  908.6 145.7 %all-reduce.2 = bf16[4096,432]{0,1:T(8,128)(2,1)} all-reduce(f32[4096,432]{0,1:T(8,128)} %fusion.15), channel_id=1, replica_groups=mesh['wide'=32,'narrow'=8] {'narrow'}, use_global_device_ids=true, to_apply=%region_10.11 | all-reduce | flops 1769472 | bytes 10616832 | tf_op jit(solution)/shard_map/psum | solution.py:93
  1054.4 6.4 copy.100
  1060.7 7.0 reshape.196
  1067.7 5.6 multiply_reduce_fusion
  (68 shorter events, 29.4 us)
Async XLA Ops:
  6.5 890.3 %copy-start = (bf16[1728,432]{0,1:T(8,128)(2,1)S(1)}, bf16[1728,432]{0,1:T(8,128)(2,1)}, u32[]{:S(2)}) copy-start(bf16[1728,432]{0,1:T(8,128)(2,1)} %param.17) | copy-start | bytes 4478980
  6.5 36.0 %copy-start.6 = (f32[5120]{0:T(1024)S(1)}, f32[5120]{0:T(1024)}, u32[]{:S(2)}) copy-start(f32[5120]{0:T(1024)} %param.10) | copy-start | bytes 61444
  6.5 43.0 %copy-start.2 = (bf16[2048,160]{0,1:T(8,128)(2,1)S(1)}, bf16[2048,160]{0,1:T(8,128)(2,1)}, u32[]{:S(2)}) copy-start(bf16[2048,160]{0,1:T(8,128)(2,1)} %param.11) | copy-start | bytes 1966084
  35.8 13.5 %all-to-all-start.1 = ((f32[32,1,1024]{2,1,0:T(1,128)}), f32[32,1,1024]{2,1,0:T(1,128)S(1)}, u32[]{:S(2)}, u32[]{:S(2)}) async-start(f32[32,1,1024]{2,1,0:T(1,128)} %broadcast_in_dim.40), calls=%async_computation.1 | async-start | bytes 262144 | tf_op jit(solution)/shard_map/all_to_all | solution.py:13
  42.5 131.2 %reduce-scatter.2.cloned.1.call-start = ((), (), s32[]{:S(2)}) async-start(), calls=%async_computation.7 | async-start | bytes 8650752 | tf_op jit(solution)/shard_map/reduce_scatter | solution.py:51
  54.1 143.0 %copy-start.7 = (s32[1024,4]{0,1:T(4,128)S(1)}, s32[1024,4]{0,1:T(4,128)}, u32[]{:S(2)}) copy-start(s32[1024,4]{0,1:T(4,128)} %param.12) | copy-start | bytes 49156
  54.1 200.1 %all-gather.5.cloned.1.call-start = ((), (), s32[]{:S(2)}) async-start(), calls=%async_computation.8 | async-start | bytes 4325376 | tf_op jit(solution)/shard_map/all_gather | solution.py:59
  196.5 292.7 %all-gather.7.cloned.1.call-start = ((), (), s32[]{:S(2)}) async-start(), calls=%async_computation.9 | async-start | bytes 23592960 | tf_op jit(solution)/shard_map/all_gather | solution.py:70
  277.6 372.2 %all-gather.9.cloned.1.call-start = ((), (), s32[]{:S(2)}) async-start(), calls=%async_computation.10 | async-start | bytes 18923520 | tf_op jit(solution)/shard_map/all_gather | solution.py:82
  508.8 9.5 copy-start.1
  508.8 101.0 %all-to-all-start.4 = ((f32[32,128,160]{1,2,0:T(8,128)}), f32[32,128,160]{1,2,0:T(8,128)}, u32[]{:S(2)}, u32[]{:S(2)}) async-start(f32[32,128,160]{1,2,0:T(8,128)} %copy.96), calls=%async_computation.5 | async-start | bytes 5242880 | tf_op jit(solution)/shard_map/all_to_all | solution.py:71
  518.0 378.9 %all-gather.11.cloned.1.call-start = ((), (), s32[]{:S(2)}) async-start(), calls=%async_computation.11 | async-start | bytes 15138816 | tf_op jit(solution)/shard_map/all_gather | solution.py:89
  520.5 5.6 copy-start.5
  628.1 32.1 %copy-start.3 = (bf16[32,5120]{1,0:T(8,128)(2,1)S(1)}, bf16[32,5120]{1,0:T(8,128)(2,1)}, u32[]{:S(2)}) copy-start(bf16[32,5120]{1,0:T(8,128)(2,1)} %param.13) | copy-start | bytes 983044
  658.9 35.4 %copy-start.4 = (bf16[160,640]{1,0:T(8,128)(2,1)S(1)}, bf16[160,640]{1,0:T(8,128)(2,1)}, u32[]{:S(2)}) copy-start(bf16[160,640]{1,0:T(8,128)(2,1)} %param.16) | copy-start | bytes 614404
Sparse Core Ops, SparseCore 0:
  54.2 119.3 reduce-scatter.1
  196.6 57.4 all-gather.4
  277.7 211.4 all-gather.6
  491.6 158.1 all-gather.8
  660.3 119.0 all-gather.10
